TPU v7x, 32 devices: a whole 2x2x4 slice. The times are simulated.
32 devices in a mesh: groups: 2 (over y), blk: 4 (over z), split: 2 (over x), sub: 2 (over core).
Axes of the slice: x: 2, y: 2, z: 4, core: 2. Of those that a mesh axis runs over, the one named last changes fastest.
Arguments:
- attention_output_rows: bfloat16 [1024, 8192], P(('groups', 'blk'), 'split'), parts along dimension 0, may hold values from -6 to 6
- residual: bfloat16 [1024, 8192], P(('groups', 'split'), ('blk', 'sub')), parts along dimension 0, may hold values from -6 to 6
- output_projection_weight: bfloat16 [8192, 8192], P('split', ('blk', 'sub')), may hold values from -0.0625 to 0.0625
- down_adapter_bank: bfloat16 [4, 64, 8192], P('blk', None, 'split'), may hold values from -0.0625 to 0.0625
- up_adapter_bank: bfloat16 [4, 64, 8192], P('split', None, ('blk', 'sub')), may hold values from -0.75 to 0.75
- rollout_row_tenant: int32 [1024], P('groups'), parts along dimension 0, may hold values from 0 to 3, as said below
- tenant_bank_entry: int32 [4], replicated, may hold values from 0 to 3, each once
- tenant_live_rank: int32 [4], replicated, may hold values from 16 to 64, as said below
Outputs:
- layer_out: bfloat16 [1024, 8192], P(('groups', 'split'), ('blk', 'sub')), parts along dimension 0
There are 2 independent parts, one for each index of `groups`. A program takes and returns all parts, laid end to end along the dimension named above; an argument that names none is the same for every part. Nothing has to cross between parts.
Inputs may be any that keep to these rules, and one draw needn't show every extreme that they name: `rollout_row_tenant`: every tenant owns at least one row of every part. `tenant_live_rank`: some tenant has the full rank 64.
All inputs are finite; a program needn't handle non-finite values.
Results may differ from a plain program's by a relative error of at most 0.0038.
Values may be sent and summed in bfloat16 or wider, within the bound.
A program may use at most 64 MiB of HBM per device.

v0:
```python
import jax
import jax.numpy as jnp
from jax import lax
from jax.sharding import PartitionSpec as P


def shards(
    attention_output_rows,
    residual,
    output_projection_weight,
    down_adapter_bank,
    up_adapter_bank,
    rollout_row_tenant,
    tenant_bank_entry,
    tenant_live_rank,
):
    out_cols = output_projection_weight.shape[1]
    feat_width = attention_output_rows.shape[1]
    rank_mask_rows = down_adapter_bank.shape[1]
    gathered_down_maps = lax.all_gather(down_adapter_bank, "blk", axis=0, tiled=True)
    tenant_count = gathered_down_maps.shape[0]
    total_rows = rollout_row_tenant.shape[0]
    tenant_ids = jnp.arange(tenant_count, dtype=jnp.int32)
    tenant_hot = (rollout_row_tenant[:, None] == tenant_ids[None, :]).astype(jnp.int32)
    slot_all = jnp.sum(tenant_hot * tenant_bank_entry[None, :], axis=1)
    rank_all = jnp.sum(tenant_hot * tenant_live_rank[None, :], axis=1)
    down_cols = gathered_down_maps.reshape(tenant_count * rank_mask_rows, feat_width).T
    joined = jnp.concatenate([output_projection_weight, down_cols], axis=1)
    own_count = total_rows // lax.axis_size("split")
    own_start = lax.axis_index("split") * own_count
    own_slot = lax.dynamic_slice_in_dim(slot_all, own_start, own_count, 0)
    own_rank = lax.dynamic_slice_in_dim(rank_all, own_start, own_count, 0)
    own_hot = own_slot[:, None] == tenant_ids[None, :]
    full = jnp.dot(
        lax.all_gather(attention_output_rows, "blk", axis=0, tiled=True),
        joined,
        preferred_element_type=jnp.float32,
    )
    piece_hot = slot_all[:, None] == tenant_ids[None, :]
    values = full[:, out_cols:]
    shaped = values.reshape(values.shape[0], tenant_count, rank_mask_rows)
    products = jnp.concatenate(
        [
            full[:, :out_cols],
            jnp.sum(jnp.where(piece_hot[:, :, None], shaped, jnp.zeros((), jnp.float32)), axis=1),
        ],
        axis=1,
    )
    summed = lax.psum_scatter(products, "split", scatter_dimension=0, tiled=True)
    frozen_output_term = summed[:, :out_cols]
    low_rank = summed[:, out_cols:]
    gathered_up_maps = lax.all_gather(up_adapter_bank, "split", axis=0, tiled=True)
    kept_mask = jnp.arange(rank_mask_rows, dtype=jnp.int32)[None, :] < own_rank[:, None]
    scaling = rank_mask_rows / own_rank.astype(jnp.float32)
    low_scaled = jnp.where(
        kept_mask, low_rank * scaling[:, None], jnp.zeros((), jnp.float32)
    ).astype(jnp.bfloat16)
    rank_expanded_rows = jnp.where(
        own_hot[:, :, None], low_scaled[:, None, :], jnp.zeros((), jnp.bfloat16)
    ).reshape(own_count, tenant_count * rank_mask_rows)
    adapter_output_term = jnp.dot(
        rank_expanded_rows,
        gathered_up_maps.reshape(tenant_count * rank_mask_rows, out_cols),
        preferred_element_type=jnp.float32,
    )
    return (residual.astype(jnp.float32) + frozen_output_term + adapter_output_term).astype(
        jnp.bfloat16
    )


def solution(mesh):
    in_specs = (
        P(("groups", "blk"), "split"),
        P(("groups", "split"), ("blk", "sub")),
        P("split", ("blk", "sub")),
        P("blk", None, "split"),
        P("split", None, ("blk", "sub")),
        P("groups"),
        P(),
        P(),
    )
    out_specs = P(("groups", "split"), ("blk", "sub"))
    return jax.shard_map(shards, mesh=mesh, in_specs=in_specs, out_specs=out_specs, check_vma=False)
```

profile of v0, /device:TPU:0, one launch (start us, length us, event | category | flops | bytes accessed | tf_op | source)
XLA Modules:
  0.0 194.9 jit_solution(4081771632402627207)
XLA Ops:
  6.5 0.0 all-gather.3.cloned.1.call-start
  6.5 0.7 all-gather.3.cloned.1.call-update
  7.3 0.0 all-gather.5.cloned.1.call-start
  7.3 0.7 all-gather.5.cloned.1.call-update
  8.0 0.0 reduce-scatter.2.cloned.1.call-start
  8.1 0.8 select_reduce_fusion.1
  8.8 48.5 %all-gather.3.cloned.1.call-done = bf16[4,64,4096]{2,1,0:T(8,128)(2,1)} async-done(((bf16[1,64,4096]{2,1,0:T(8,128)(2,1)}), bf16[4,64,4096]{2,1,0:T(8,128)(2,1)}) %all-gather.3.cloned.1.call-update) | async-done | bytes 2097168 | tf_op jit(solution)/shard_map/all_gather | solution.py:20
  57.3 3.3 %copy.18 = bf16[256,4096]{0,1:T(8,128)(2,1)S(1)} copy(bf16[256,4096]{1,0:T(8,128)(2,1)} %bitcast.14) | data formatting | bytes 4194304 | tf_op jit(solution)/shard_map/reshape | solution.py:27
  60.6 77.9 %all-gather.5.cloned.1.call-done = bf16[512,4096]{1,0:T(8,128)(2,1)} async-done(((bf16[128,4096]{1,0:T(8,128)(2,1)}), bf16[512,4096]{1,0:T(8,128)(2,1)}) %all-gather.5.cloned.1.call-update) | async-done | bytes 4194320 | tf_op jit(solution)/shard_map/all_gather | solution.py:35
  138.5 9.7 %fusion.4 = f32[512,1280]{0,1:T(8,128)S(1)} fusion(bf16[512,4096]{1,0:T(8,128)(2,1)} %all-gather.5.cloned.1.call-done, bf16[4096,256]{1,0:T(8,128)(2,1)S(1)} %bitcast.15, bf16[4096,1024]{1,0:T(8,128)(2,1)} %param.10), kind=kOutput, calls=%fused_computation.4 | convolution fusion | flops 5389680640 | bytes 17301504 | tf_op jit(solution)/shard_map/dot_general | solution.py:34
  148.2 0.2 slice.16
  148.4 0.1 select_reduce_fusion
  148.5 0.0 copy-start
  148.5 1.6 pad_maximum_fusion
  150.0 0.0 copy-start.1
  150.0 0.0 reduce-scatter.2.cloned.1.call-update
  150.1 0.1 dynamic_slice.6
  150.1 0.0 copy-done
  150.1 0.2 copy.17
  150.4 0.1 convert_divide_fusion
  150.4 0.5 copy-done.1
  151.0 12.9 %all_gather.11 = bf16[4,64,1024]{2,1,0:T(8,128)(2,1)S(1)} all-gather(bf16[2,64,1024]{2,1,0:T(8,128)(2,1)S(1)} %copy-done.1), channel_id=1, replica_groups=mesh['groups'=2,'blk'=4,'split'=2,'sub'=2] {'split'}, dimensions={0}, use_global_device_ids=true | all-gather | bytes 786432 | tf_op jit(solution)/shard_map/all_gather | solution.py:52
  163.9 21.1 %reduce-scatter.2.cloned.1.call-done = f32[256,1088]{0,1:T(8,128)} async-done(((f32[512,1088]{0,1:T(8,128)}), f32[256,1088]{0,1:T(8,128)}) %reduce-scatter.2.cloned.1.call-update) | async-done | bytes 1114128 | tf_op jit(solution)/shard_map/reduce_scatter | solution.py:49
  185.0 0.9 fusion.12
  185.8 1.6 fusion.8
  187.4 1.0 copy.20
  (3 shorter events, 0.1 us)
Async XLA Ops:
  6.5 50.8 %all-gather.3.cloned.1.call-start = ((), (), s32[]{:S(2)}) async-start(), calls=%async_computation.1 | async-start | bytes 2621440 | tf_op jit(solution)/shard_map/all_gather | solution.py:20
  7.3 131.2 %all-gather.5.cloned.1.call-start = ((), (), s32[]{:S(2)}) async-start(), calls=%async_computation.2 | async-start | bytes 5242880 | tf_op jit(solution)/shard_map/all_gather | solution.py:35
  8.0 177.0 %reduce-scatter.2.cloned.1.call-start = ((), (), s32[]{:S(2)}) async-start(), calls=%async_computation.3 | async-start | bytes 3342336 | tf_op jit(solution)/shard_map/reduce_scatter | solution.py:49
  148.5 1.7 copy-start
  150.0 0.9 copy-start.1
Sparse Core Ops, SparseCore 0:
  8.9 48.3 all-gather.2
  58.9 79.5 all-gather.4
  150.2 34.7 reduce-scatter.1
where the time goes:
time: 195 us
  waiting for transfers between devices  149 us (76%)
  between operations  13.2 us (7%)
  blocking collectives  12.9 us (7%)
  matrix products  11.3 us (6%)
  local copies, waits for them, and re-layouts  5.31 us (3%)
  other arithmetic  3.35 us (2%)
    all_gather x1, waiting for transfers between devices, shards(): lax.all_gather(attention_output_rows, 'blk', axis=0, tiled=True)  77.9 us
    all_gather x1, waiting for transfers between devices, shards(): lax.all_gather(down_adapter_bank, 'blk', axis=0, tiled=True)  48.5 us
    reduce_scatter x1, waiting for transfers between devices, shards(): lax.psum_scatter(products, 'split', scatter_dimension=0, tiled=True)  21.1 us
    all_gather x1, blocking collectives, shards(): lax.all_gather(up_adapter_bank, 'split', axis=0, tiled=True)  12.9 us
    dot_general x1, matrix products, shards(): jnp.dot(lax.all_gather(attention_output_rows, 'blk', axis=0, tiled=True),...  9.71 us
  transfers between devices with their start and end apart: 3, of which 3 were waited for; matrix products, arithmetic and copies ran while one was open for 2% of the time, Pallas kernels for 0%

commit v1 on v0

v1 whole, which is shorter than its diff:
```python
import functools

import jax
import jax.numpy as jnp
from jax import lax
from jax.experimental import pallas as pl
from jax.experimental.pallas import tpu as pltpu
from jax.sharding import PartitionSpec as P

CHUNK_ROWS = 32
MESH = pl.DeviceIdType.MESH


def kernel(
    nb, ns, nu, rc,
    ent_ref, rank_ref, x_ref, r_ref, w_ref, dn_ref, up_ref, ten_ref, o_ref,
    xall, wv, rv, dnp, upp, mtab, acc, lacc, xs, ls, xr, lr, lowx,
    sem_loc, sem_own, zsend, zrecv, csend, crecv, usend, urecv,
    xsend, xrecv, lsend, lrecv, gsend, grecv,
):
    blk, split, sub = lax.axis_index("blk"), lax.axis_index("split"), lax.axis_index("sub")
    rows, feats = x_ref.shape
    cols = w_ref.shape[1]
    own = r_ref.shape[0]
    banks, rank = dn_ref.shape[0], dn_ref.shape[1]
    up_banks = up_ref.shape[0]
    wide = dnp.shape[0]
    total = ten_ref.shape[1]
    tenants = ent_ref.shape[0]
    nc = rows // rc
    half = rc // nu

    w_copy = pltpu.make_async_copy(w_ref, wv, sem_loc.at[0])
    w_copy.start()
    x_copy = pltpu.make_async_copy(
        x_ref, xall.at[pl.ds(pl.multiple_of(blk * rows, rows), rows)], sem_own
    )
    x_copy.start()
    loads = [pltpu.make_async_copy(r_ref, rv, sem_loc.at[1])]
    for e in range(banks):
        loads.append(
            pltpu.make_async_copy(dn_ref.at[e], dnp.at[pl.ds(e * rank, rank)], sem_loc.at[2 + e])
        )

    def up_slot(bank):
        return upp.at[bank // banks, pl.ds(pl.multiple_of(bank % banks * rank, rank), rank)]

    for e in range(up_banks):
        loads.append(
            pltpu.make_async_copy(
                up_ref.at[e], up_slot(split * up_banks + e), sem_loc.at[2 + banks + e]
            )
        )
    for load in loads:
        load.start()

    barrier = pltpu.get_barrier_semaphore()
    for k in range(1, nb):
        pl.semaphore_signal(
            barrier, inc=1, device_id={"blk": lax.rem(blk + k, nb)}, device_id_type=MESH
        )
    for k in range(1, ns):
        pl.semaphore_signal(
            barrier, inc=1, device_id={"split": lax.rem(split + k, ns)}, device_id_type=MESH
        )
    for k in range(1, nu):
        pl.semaphore_signal(
            barrier, inc=1, device_id={"sub": lax.rem(sub + k, nu)}, device_id_type=MESH
        )
    pl.semaphore_wait(barrier, nb + ns + nu - 3)

    def half_rows(ref, b, j, core):
        start = pl.multiple_of(b * rows + j * rc + core * half, half)
        return ref.at[pl.ds(start, half)]

    def z_copy(b, j, side, src=None):
        dst = half_rows(xall, b, j, sub)
        return pltpu.make_async_remote_copy(
            src_ref=dst if src is None else src,
            dst_ref=dst,
            send_sem=zsend.at[side, b * nc + j],
            recv_sem=zrecv.at[b * nc + j],
            device_id={"blk": lax.rem(blk + 1 - 2 * side + nb, nb)},
            device_id_type=MESH,
        )

    def c_copy(b, j, k, core):
        piece = half_rows(xall, b, j, core)
        return pltpu.make_async_remote_copy(
            src_ref=piece,
            dst_ref=piece,
            send_sem=csend.at[k - 1, b * nc + j],
            recv_sem=crecv.at[k - 1, b * nc + j],
            device_id={"sub": lax.rem(sub + k, nu)},
            device_id_type=MESH,
        )

    for j in range(nc):
        src = x_ref.at[pl.ds(pl.multiple_of(j * rc + sub * half, half), half)]

        @pl.when(blk < nb - 1)
        def _():
            z_copy(blk, j, 0, src).start()

        @pl.when(blk > 0)
        def _():
            z_copy(blk, j, 1, src).start()

    def u_copy(k, e, owner):
        return pltpu.make_async_remote_copy(
            src_ref=up_ref.at[e],
            dst_ref=up_slot(owner * up_banks + e),
            send_sem=usend.at[k - 1, e],
            recv_sem=urecv.at[k - 1, e],
            device_id={"split": lax.rem(split + k, ns)},
            device_id_type=MESH,
        )

    for k in range(1, ns):
        for e in range(up_banks):
            u_copy(k, e, split).start()

    if wide > banks * rank:
        pad = wide - banks * rank
        dnp[pl.ds(banks * rank, pad), :] = jnp.zeros((pad, feats), dnp.dtype)
        for p in range(nb):
            upp[p, pl.ds(banks * rank, pad), :] = jnp.zeros((pad, cols), upp.dtype)
    lane = lax.broadcasted_iota(jnp.int32, (1, wide), 1)
    tcol = jnp.transpose(
        jnp.broadcast_to(ten_ref[...].astype(jnp.float32), (8, total))
    )[:, :1]
    table = jnp.zeros((total, wide), jnp.float32)
    for t in range(tenants):
        live = jnp.full((1, wide), rank_ref[t], jnp.int32)
        slot = jnp.full((1, wide), ent_ref[t], jnp.int32)
        line = jnp.zeros((1, wide), jnp.float32)
        for e in range(banks):
            keep = (
                (lane >= e * rank) & (lane < e * rank + jnp.minimum(live, rank))
                & (slot == blk * banks + e)
            )
            line = jnp.where(keep, rank / live.astype(jnp.float32), line)
        table = jnp.where(tcol == t, line, table)
    mtab[...] = table

    for load in loads:
        load.wait()
    x_copy.wait()
    w_copy.wait()

    def x_pair(xo, b, j, src_split, count=2):
        start = pl.multiple_of(b * rows + j * rc, rc)
        dest = pl.multiple_of(b * rows + j * rc - xo * own, rc)
        chunk, mine = b * nc + j, (b * rows + j * rc - xo * own) // rc
        pairs = ((ls, lr, lsend, lrecv), (xs, xr, xsend, xrecv))
        return [
            pltpu.make_async_remote_copy(
                src_ref=src.at[pl.ds(start, rc)],
                dst_ref=dst.at[src_split, pl.ds(dest, rc)],
                send_sem=ss.at[chunk],
                recv_sem=rs.at[src_split, mine],
                device_id={"split": xo},
                device_id_type=MESH,
            )
            for src, dst, ss, rs in pairs[:count]
        ]

    def g_copy(k, o):
        piece = lowx.at[blk, pl.ds(pl.multiple_of(o * rc, rc), rc)]
        return pltpu.make_async_remote_copy(
            src_ref=piece,
            dst_ref=piece,
            send_sem=gsend.at[k - 1, o],
            recv_sem=grecv.at[k - 1, o],
            device_id={"blk": lax.rem(blk + k, nb)},
            device_id_type=MESH,
        )

    def place(i):
        d, j, side = i // (2 * nc), i // 2 % nc, i % 2
        b = jnp.where(side == 0, blk - d, blk + d)
        valid = (b >= 0) & (b < nb) & ((d > 0) | (side == 0))
        return d, j, side, jnp.clip(b, 0, nb - 1), valid

    steps = 2 * nb * nc

    def arrive(i):
        d, j, side, b, valid = place(i)

        @pl.when(valid & (d > 0) & (i < steps))
        def _():
            z_copy(b, j, side).wait_recv()

            @pl.when((side == 0) & (blk < nb - 1))
            def _():
                z_copy(b, j, 0).start()

            @pl.when((side == 1) & (blk > 0))
            def _():
                z_copy(b, j, 1).start()

            for k in range(1, nu):
                c_copy(b, j, k, sub).start()

    def compute(i):
        d, j, side, b, valid = place(i)

        @pl.when(valid & (i >= 0) & (i < steps))
        def _():
            @pl.when(d > 0)
            def _():
                for k in range(1, nu):
                    c_copy(b, j, k, lax.rem(sub - k + nu, nu)).wait_recv()

            start = pl.multiple_of(b * rows + j * rc, rc)
            xo = (b * rows + j * rc) // own
            piece = xall[pl.ds(start, rc), :]
            low = lax.dot_general(
                piece, dnp[...], (((1,), (1,)), ((), ())), preferred_element_type=jnp.float32
            )
            part = jnp.dot(piece, wv[...], preferred_element_type=jnp.float32)

            @pl.when(xo == split)
            def _():
                at = pl.ds(pl.multiple_of(b * rows + j * rc - xo * own, rc), rc)
                lacc[at, :] = low
                acc[at, :] = part

            @pl.when(xo != split)
            def _():
                ls[pl.ds(start, rc), :] = low
                xs[pl.ds(start, rc), :] = part.astype(xs.dtype)
                for copy in x_pair(xo, b, j, split):
                    copy.start()

    def settle(i):
        d, j, side, b, valid = place(i)
        xo = (b * rows + j * rc) // own

        @pl.when(valid & (i >= 0) & (i < steps) & (xo == split))
        def _():
            o = (b * rows + j * rc - xo * own) // rc
            at = pl.ds(pl.multiple_of(o * rc, rc), rc)
            start = pl.multiple_of(b * rows + j * rc, rc)
            low = lacc[at, :]
            for k in range(1, ns):
                src = lax.rem(split + k, ns)
                x_pair(xo, b, j, src, 1)[0].wait_recv()
                low = low + lr[src, at, :]
            lowx[blk, at, :] = (low * mtab[pl.ds(start, rc), :]).astype(lowx.dtype)
            for k in range(1, nb):
                g_copy(k, o).start()

    @pl.loop(0, steps + 4)
    def _(i):
        arrive(i)
        compute(i - 2)
        settle(i - 4)

    for k in range(1, ns):
        for e in range(up_banks):
            u_copy(k, e, lax.rem(split - k + ns, ns)).wait_recv()

    @pl.loop(0, own // rc)
    def _(o):
        at = pl.ds(pl.multiple_of(o * rc, rc), rc)
        value = rv[at, :].astype(jnp.float32) + acc[at, :]
        for k in range(1, ns):
            src = lax.rem(split + k, ns)
            pltpu.make_async_remote_copy(
                src_ref=xs.at[at],
                dst_ref=xr.at[src, at],
                send_sem=xsend.at[o],
                recv_sem=xrecv.at[src, o],
                device_id={"split": src},
                device_id_type=MESH,
            ).wait_recv()
            value = value + xr[src, at, :].astype(jnp.float32)
        for k in range(1, nb):
            g_copy(k, o).wait_recv()
        for p in range(nb):
            value = value + jnp.dot(lowx[p, at, :], upp[p], preferred_element_type=jnp.float32)
        o_ref[at, :] = value.astype(o_ref.dtype)

    for k in range(1, ns):
        for e in range(up_banks):
            u_copy(k, e, split).wait_send()

    @pl.loop(0, own // rc)
    def _(o):
        for k in range(1, nb):
            g_copy(k, o).wait_send()

    @pl.loop(0, nb * nc)
    def _(n):
        b, j = n // nc, n % nc
        xo = (b * rows + j * rc) // own

        @pl.when(xo != split)
        def _():
            for copy in x_pair(xo, b, j, split):
                copy.wait_send()

        @pl.when((b <= blk) & (blk < nb - 1))
        def _():
            z_copy(b, j, 0).wait_send()

        @pl.when((b >= blk) & (blk > 0))
        def _():
            z_copy(b, j, 1).wait_send()

        @pl.when(b != blk)
        def _():
            for k in range(1, nu):
                c_copy(b, j, k, sub).wait_send()


def shards(
    nb, ns, nu,
    attention_output_rows,
    residual,
    output_projection_weight,
    down_adapter_bank,
    up_adapter_bank,
    rollout_row_tenant,
    tenant_bank_entry,
    tenant_live_rank,
):
    rows, feats = attention_output_rows.shape
    own, cols = residual.shape
    banks, rank, _ = down_adapter_bank.shape
    up_banks = up_adapter_bank.shape[0]
    total = rollout_row_tenant.shape[0]
    wide = -(-banks * rank // 128) * 128
    rc = CHUNK_ROWS
    chunks = total // rc
    dma = pltpu.SemaphoreType.DMA
    bf16, f32 = jnp.bfloat16, jnp.float32
    any_spec = pl.BlockSpec(memory_space=pl.ANY)
    smem = pl.BlockSpec(memory_space=pltpu.SMEM)
    vmem = pl.BlockSpec(memory_space=pltpu.VMEM)
    return pl.pallas_call(
        functools.partial(kernel, nb, ns, nu, rc),
        out_shape=jax.ShapeDtypeStruct((own, cols), bf16),
        in_specs=[smem, smem] + [any_spec] * 5 + [vmem],
        out_specs=vmem,
        scratch_shapes=[
            pltpu.VMEM((total, feats), bf16),
            pltpu.VMEM((feats, cols), bf16),
            pltpu.VMEM((own, cols), bf16),
            pltpu.VMEM((wide, feats), bf16),
            pltpu.VMEM((nb, wide, cols), bf16),
            pltpu.VMEM((total, wide), f32),
            pltpu.VMEM((own, cols), f32),
            pltpu.VMEM((own, wide), f32),
            pltpu.VMEM((total, cols), bf16),
            pltpu.VMEM((total, wide), f32),
            pltpu.VMEM((ns, own, cols), bf16),
            pltpu.VMEM((ns, own, wide), f32),
            pltpu.VMEM((nb, own, wide), bf16),
            dma((2 + banks + up_banks,)),
            dma,
            dma((2, chunks)),
            dma((chunks,)),
            dma((nu - 1, chunks)),
            dma((nu - 1, chunks)),
            dma((ns - 1, up_banks)),
            dma((ns - 1, up_banks)),
            dma((chunks,)),
            dma((ns, own // rc)),
            dma((chunks,)),
            dma((ns, own // rc)),
            dma((nb - 1, own // rc)),
            dma((nb - 1, own // rc)),
        ],
        compiler_params=pltpu.CompilerParams(
            collective_id=0, has_side_effects=True, vmem_limit_bytes=48 * 1024 * 1024
        ),
    )(
        tenant_bank_entry,
        tenant_live_rank,
        attention_output_rows,
        residual,
        output_projection_weight,
        down_adapter_bank,
        up_adapter_bank,
        rollout_row_tenant.reshape(1, total),
    )


def solution(mesh):
    in_specs = (
        P(("groups", "blk"), "split"),
        P(("groups", "split"), ("blk", "sub")),
        P("split", ("blk", "sub")),
        P("blk", None, "split"),
        P("split", None, ("blk", "sub")),
        P("groups"),
        P(),
        P(),
    )
    out_specs = P(("groups", "split"), ("blk", "sub"))
    body = functools.partial(
        shards, mesh.shape["blk"], mesh.shape["split"], mesh.shape["sub"]
    )
    return jax.shard_map(body, mesh=mesh, in_specs=in_specs, out_specs=out_specs, check_vma=False)
```

time: 195 us -> 66.3 us (0.34)
  waiting for transfers between devices: 149 us -> 0 us
  Pallas kernels: 0 us -> 58.9 us
  between operations: 13.2 us -> 0.02 us
  blocking collectives: 12.9 us -> 0 us
  matrix products: 11.3 us -> 0 us
  other arithmetic: 3.35 us -> 0 us
    all_gather x2 -> x0, waiting for transfers between devices: 126 us -> none  [the longest x1 77.9 us: shards(): lax.all_gather(attention_output_rows, 'blk', axis=0, tiled=True)]
    pallas_call x0 -> x1, Pallas kernels: none -> 58.9 us  [shards(): pl.pallas_call(functools.partial(kernel, nb, ns, nu, rc), out_shape=jax.S...]
    reduce_scatter x1 -> x0, waiting for transfers between devices: 21.1 us -> none  [shards(): lax.psum_scatter(products, 'split', scatter_dimension=0, tiled=True)]
    all_gather x1 -> x0, blocking collectives: 12.9 us -> none  [shards(): lax.all_gather(up_adapter_bank, 'split', axis=0, tiled=True)]
    dot_general x2 -> x0, matrix products: 11.3 us -> none  [the longest x1 9.71 us: shards(): jnp.dot(lax.all_gather(attention_output_rows, 'blk', axis=0, tiled=True),...]
    unnamed x5 -> x15, local copies, waits for them, and re-layouts: 0.76 us -> 7.04 us
    reshape x1 -> x0, local copies, waits for them, and re-layouts: 3.27 us -> none  [shards(): gathered_down_maps.reshape(tenant_count * rank_mask_rows, feat_width)]
  transfers between devices with their start and end apart: 3 -> 0, of which waited for: 3 -> 0; matrix products, arithmetic and copies ran while one was open for 2% -> 0% of each run, Pallas kernels for 0% -> 0%
where the time goes in v1:
time: 66.3 us; the launch traced here: 66 us
  Pallas kernels  58.9 us (89%)
  local copies, waits for them, and re-layouts  7.04 us (11%)
    pallas_call x1, Pallas kernels, shards(): pl.pallas_call(functools.partial(kernel, nb, ns, nu, rc), out_shape=jax.S...  58.9 us
    unnamed x15, local copies, waits for them, and re-layouts  7.04 us

profile of v1, /device:TPU:0, one launch (start us, length us, event | category | flops | bytes accessed | tf_op | source)
XLA Modules:
  0.0 66.0 jit_solution(16137012823693084234)
XLA Ops:
  0.0 0.0 copy-start
  0.0 1.2 %copy-done = bf16[128,4096]{1,0:T(8,128)(2,1)S(1)} copy-done((bf16[128,4096]{1,0:T(8,128)(2,1)S(1)}, bf16[128,4096]{1,0:T(8,128)(2,1)}, u32[]{:S(2)}) %copy-start) | copy-done | bytes 1048600
  1.2 0.0 copy-start.1
  1.2 1.0 %copy-done.1 = bf16[256,1024]{1,0:T(8,128)(2,1)S(1)} copy-done((bf16[256,1024]{1,0:T(8,128)(2,1)S(1)}, bf16[256,1024]{1,0:T(8,128)(2,1)}, u32[]{:S(2)}) %copy-start.1) | copy-done | bytes 524312
  2.3 0.0 copy-start.2
  2.3 1.0 %copy-done.2 = bf16[1,64,4096]{2,1,0:T(8,128)(2,1)S(1)} copy-done((bf16[1,64,4096]{2,1,0:T(8,128)(2,1)S(1)}, bf16[1,64,4096]{2,1,0:T(8,128)(2,1)}, u32[]{:S(2)}) %copy-start.2) | copy-done | bytes 524312
  3.3 0.0 copy-start.3
  3.3 0.9 %copy-done.3 = bf16[2,64,1024]{2,1,0:T(8,128)(2,1)S(1)} copy-done((bf16[2,64,1024]{2,1,0:T(8,128)(2,1)S(1)}, bf16[2,64,1024]{2,1,0:T(8,128)(2,1)}, u32[]{:S(2)}) %copy-start.3) | copy-done | bytes 262168
  4.3 0.0 copy-start.4
  4.3 0.7 %copy-done.4 = s32[512]{0:T(512)S(1)} copy-done((s32[512]{0:T(512)S(1)}, s32[512]{0:T(512)}, u32[]{:S(2)}) %copy-start.4) | copy-done | bytes 2072
  4.9 0.0 copy-start.5
  4.9 0.7 copy-done.5
  5.6 0.0 copy-start.6
  5.6 0.7 copy-done.6
  6.3 58.9 %shard_map.82 = bf16[256,1024]{1,0:T(8,128)(2,1)S(1)} custom-call(s32[4]{0:T(128)S(1)} %copy-done.5, s32[4]{0:T(128)S(1)} %copy-done.6, bf16[128,4096]{1,0:T(8,128)(2,1)S(1)} %copy-done, bf16[256,1024]{1,0:T(8,128)(2,1)S(1)} %copy-done.1, bf16[4096,1024]{1,0:T(8,128)(2,1)} %w_ref.1, bf16[1,64,4096]{2,1,0:T(8,128)(2,1)S(1)} %copy-done.2, ...), custom_call_target="tpu_custom_call" | custom-call | tf_op jit(solution)/shard_map/pallas_call | solution.py:342
  65.2 0.8 %copy.10 = bf16[256,1024]{1,0:T(8,128)(2,1)} copy(bf16[256,1024]{1,0:T(8,128)(2,1)S(1)} %shard_map.82) | data formatting | bytes 1048576
Async XLA Ops:
  0.0 1.2 %copy-start = (bf16[128,4096]{1,0:T(8,128)(2,1)S(1)}, bf16[128,4096]{1,0:T(8,128)(2,1)}, u32[]{:S(2)}) copy-start(bf16[128,4096]{1,0:T(8,128)(2,1)} %x_ref.1) | copy-start | bytes 3145732
  1.2 1.0 %copy-start.1 = (bf16[256,1024]{1,0:T(8,128)(2,1)S(1)}, bf16[256,1024]{1,0:T(8,128)(2,1)}, u32[]{:S(2)}) copy-start(bf16[256,1024]{1,0:T(8,128)(2,1)} %r_ref.1) | copy-start | bytes 1572868
  2.3 1.0 %copy-start.2 = (bf16[1,64,4096]{2,1,0:T(8,128)(2,1)S(1)}, bf16[1,64,4096]{2,1,0:T(8,128)(2,1)}, u32[]{:S(2)}) copy-start(bf16[1,64,4096]{2,1,0:T(8,128)(2,1)} %dn_ref.1) | copy-start | bytes 1572868
  3.3 0.9 %copy-start.3 = (bf16[2,64,1024]{2,1,0:T(8,128)(2,1)S(1)}, bf16[2,64,1024]{2,1,0:T(8,128)(2,1)}, u32[]{:S(2)}) copy-start(bf16[2,64,1024]{2,1,0:T(8,128)(2,1)} %up_ref.1) | copy-start | bytes 786436
  4.3 0.7 %copy-start.4 = (s32[512]{0:T(512)S(1)}, s32[512]{0:T(512)}, u32[]{:S(2)}) copy-start(s32[512]{0:T(512)} %param.13) | copy-start | bytes 6148
  4.9 0.7 copy-start.5
  5.6 0.7 copy-start.6

commit v2 on v1

--- a/solution.py
+++ b/solution.py
@@ -7,7 +7,7 @@
 from jax.experimental.pallas import tpu as pltpu
 from jax.sharding import PartitionSpec as P
 
-CHUNK_ROWS = 32
+CHUNK_ROWS = 64
 MESH = pl.DeviceIdType.MESH
 
 
@@ -374,7 +374,7 @@
             dma((nb - 1, own // rc)),
         ],
         compiler_params=pltpu.CompilerParams(
-            collective_id=0, has_side_effects=True, vmem_limit_bytes=48 * 1024 * 1024
+            collective_id=0, has_side_effects=True
         ),
     )(
         tenant_bank_entry,

time: 66.3 us -> 60.1 us (0.906)
  local copies, waits for them, and re-layouts: 7.04 us -> 1.87 us
  Pallas kernels: 58.9 us -> 58 us
    unnamed x15 -> x1, local copies, waits for them, and re-layouts: 7.04 us -> 1.87 us
    pallas_call x1, Pallas kernels: 58.9 us -> 58 us  [shards(): pl.pallas_call(functools.partial(kernel, nb, ns, nu, rc), out_shape=jax.S...]
where the time goes in v2:
time: 60.1 us; the launch traced here: 59.9 us
  Pallas kernels  58 us (97%)
  local copies, waits for them, and re-layouts  1.87 us (3%)
    pallas_call x1, Pallas kernels, shards(): pl.pallas_call(functools.partial(kernel, nb, ns, nu, rc), out_shape=jax.S...  58 us
    unnamed x1, local copies, waits for them, and re-layouts  1.87 us

profile of v2, /device:TPU:0, one launch (start us, length us, event | category | flops | bytes accessed | tf_op | source)
XLA Modules:
  0.0 59.9 jit_solution(13562047640290591496)
XLA Ops:
  0.0 58.0 %shard_map.82 = bf16[256,1024]{1,0:T(8,128)(2,1)} custom-call(s32[4]{0:T(128)} %ent_ref.1, s32[4]{0:T(128)} %rank_ref.1, bf16[128,4096]{1,0:T(8,128)(2,1)} %x_ref.1, bf16[256,1024]{1,0:T(8,128)(2,1)} %r_ref.1, bf16[4096,1024]{1,0:T(8,128)(2,1)} %w_ref.1, bf16[1,64,4096]{2,1,0:T(8,128)(2,1)} %dn_ref.1, bf16[2,64,1024]{2,1,0:T(8,128)(2,1)} %up_ref.1, ...), custom_call_target="tpu_custom_call" | custom-call | tf_op jit(solution)/shard_map/pallas_call | solution.py:342
  58.0 1.9 %copy.10 = bf16[256,1024]{1,0:T(8,128)(2,1)} copy(bf16[256,1024]{1,0:T(8,128)(2,1)} %shard_map.82) | data formatting | bytes 1048576

commit v3 on v2

--- a/solution.py
+++ b/solution.py
@@ -16,7 +16,7 @@
     ent_ref, rank_ref, x_ref, r_ref, w_ref, dn_ref, up_ref, ten_ref, o_ref,
     xall, wv, rv, dnp, upp, mtab, acc, lacc, xs, ls, xr, lr, lowx,
     sem_loc, sem_own, zsend, zrecv, csend, crecv, usend, urecv,
-    xsend, xrecv, lsend, lrecv, gsend, grecv,
+    xsend, xrecv, lsend, lrecv, gsend, grecv, fsend, frecv, bsend, brecv,
 ):
     blk, split, sub = lax.axis_index("blk"), lax.axis_index("split"), lax.axis_index("sub")
     rows, feats = x_ref.shape
@@ -29,6 +29,11 @@
     tenants = ent_ref.shape[0]
     nc = rows // rc
     half = rc // nu
+    group = nb // 2
+    upper = blk // group
+    middle = group - 1 + upper
+    in_middle = blk == middle
+    share = own // nu
 
     w_copy = pltpu.make_async_copy(w_ref, wv, sem_loc.at[0])
     w_copy.start()
@@ -37,13 +42,17 @@
     )
     x_copy.start()
     loads = [pltpu.make_async_copy(r_ref, rv, sem_loc.at[1])]
-    for e in range(banks):
-        loads.append(
-            pltpu.make_async_copy(dn_ref.at[e], dnp.at[pl.ds(e * rank, rank)], sem_loc.at[2 + e])
-        )
+
+    def bank_slot(place, e):
+        return dnp.at[pl.ds(pl.multiple_of((place * banks + e) * rank, rank), rank)]
+
+    bank_loads = [
+        pltpu.make_async_copy(dn_ref.at[e], bank_slot(blk % group, e), sem_loc.at[2 + e])
+        for e in range(banks)
+    ]
 
     def up_slot(bank):
-        return upp.at[bank // banks, pl.ds(pl.multiple_of(bank % banks * rank, rank), rank)]
+        return upp.at[pl.ds(pl.multiple_of(bank * rank, rank), rank)]
 
     for e in range(up_banks):
         loads.append(
@@ -54,6 +63,11 @@
     for load in loads:
         load.start()
 
+    @pl.when(in_middle)
+    def _():
+        for load in bank_loads:
+            load.start()
+
     barrier = pltpu.get_barrier_semaphore()
     for k in range(1, nb):
         pl.semaphore_signal(
@@ -106,6 +120,21 @@
         def _():
             z_copy(blk, j, 1, src).start()
 
+    def b_copy(e, place):
+        return pltpu.make_async_remote_copy(
+            src_ref=dn_ref.at[e],
+            dst_ref=bank_slot(place, e),
+            send_sem=bsend.at[e],
+            recv_sem=brecv.at[place, e],
+            device_id={"blk": middle},
+            device_id_type=MESH,
+        )
+
+    @pl.when(jnp.logical_not(in_middle))
+    def _():
+        for e in range(banks):
+            b_copy(e, blk % group).start()
+
     def u_copy(k, e, owner):
         return pltpu.make_async_remote_copy(
             src_ref=up_ref.at[e],
@@ -120,11 +149,6 @@
         for e in range(up_banks):
             u_copy(k, e, split).start()
 
-    if wide > banks * rank:
-        pad = wide - banks * rank
-        dnp[pl.ds(banks * rank, pad), :] = jnp.zeros((pad, feats), dnp.dtype)
-        for p in range(nb):
-            upp[p, pl.ds(banks * rank, pad), :] = jnp.zeros((pad, cols), upp.dtype)
     lane = lax.broadcasted_iota(jnp.int32, (1, wide), 1)
     tcol = jnp.transpose(
         jnp.broadcast_to(ten_ref[...].astype(jnp.float32), (8, total))
@@ -134,10 +158,10 @@
         live = jnp.full((1, wide), rank_ref[t], jnp.int32)
         slot = jnp.full((1, wide), ent_ref[t], jnp.int32)
         line = jnp.zeros((1, wide), jnp.float32)
-        for e in range(banks):
+        for e in range(group * banks):
             keep = (
                 (lane >= e * rank) & (lane < e * rank + jnp.minimum(live, rank))
-                & (slot == blk * banks + e)
+                & (slot == upper * group * banks + e)
             )
             line = jnp.where(keep, rank / live.astype(jnp.float32), line)
         table = jnp.where(tcol == t, line, table)
@@ -148,31 +172,44 @@
     x_copy.wait()
     w_copy.wait()
 
-    def x_pair(xo, b, j, src_split, count=2):
+    def x_copy_of(src, dst, ss, rs, xo, b, j, src_split):
         start = pl.multiple_of(b * rows + j * rc, rc)
         dest = pl.multiple_of(b * rows + j * rc - xo * own, rc)
-        chunk, mine = b * nc + j, (b * rows + j * rc - xo * own) // rc
-        pairs = ((ls, lr, lsend, lrecv), (xs, xr, xsend, xrecv))
-        return [
-            pltpu.make_async_remote_copy(
-                src_ref=src.at[pl.ds(start, rc)],
-                dst_ref=dst.at[src_split, pl.ds(dest, rc)],
-                send_sem=ss.at[chunk],
-                recv_sem=rs.at[src_split, mine],
-                device_id={"split": xo},
-                device_id_type=MESH,
-            )
-            for src, dst, ss, rs in pairs[:count]
-        ]
-
-    def g_copy(k, o):
-        piece = lowx.at[blk, pl.ds(pl.multiple_of(o * rc, rc), rc)]
-        return pltpu.make_async_remote_copy(
-            src_ref=piece,
-            dst_ref=piece,
-            send_sem=gsend.at[k - 1, o],
-            recv_sem=grecv.at[k - 1, o],
+        return pltpu.make_async_remote_copy(
+            src_ref=src.at[pl.ds(start, rc)],
+            dst_ref=dst.at[src_split, pl.ds(dest, rc)],
+            send_sem=ss.at[b * nc + j],
+            recv_sem=rs.at[src_split, dest // rc],
+            device_id={"split": xo},
+            device_id_type=MESH,
+        )
+
+    def p_copy(*where):
+        return x_copy_of(xs, xr, xsend, xrecv, *where)
+
+    def l_copy(*where):
+        return x_copy_of(ls, lr, lsend, lrecv, *where)
+
+    def share_of(h, core):
+        return lowx.at[h, pl.ds(pl.multiple_of(core * share, share), share)]
+
+    def g_copy(k, h):
+        return pltpu.make_async_remote_copy(
+            src_ref=share_of(h, sub),
+            dst_ref=share_of(h, sub),
+            send_sem=gsend.at[k - 1],
+            recv_sem=grecv.at[h],
             device_id={"blk": lax.rem(blk + k, nb)},
+            device_id_type=MESH,
+        )
+
+    def f_copy(k, h, core):
+        return pltpu.make_async_remote_copy(
+            src_ref=share_of(h, core),
+            dst_ref=share_of(h, core),
+            send_sem=fsend.at[k - 1, h],
+            recv_sem=frecv.at[k - 1, h],
+            device_id={"sub": lax.rem(sub + k, nu)},
             device_id_type=MESH,
         )
 
@@ -215,47 +252,81 @@
             start = pl.multiple_of(b * rows + j * rc, rc)
             xo = (b * rows + j * rc) // own
             piece = xall[pl.ds(start, rc), :]
+            part = jnp.dot(piece, wv[...], preferred_element_type=jnp.float32)
+
+            @pl.when(xo == split)
+            def _():
+                at = pl.ds(pl.multiple_of(b * rows + j * rc - xo * own, rc), rc)
+                acc[at, :] = part
+
+            @pl.when(xo != split)
+            def _():
+                xs[pl.ds(start, rc), :] = part.astype(xs.dtype)
+                p_copy(xo, b, j, split).start()
+
+    @pl.loop(0, steps + 2)
+    def _(i):
+        arrive(i)
+        compute(i - 2)
+
+    @pl.when(in_middle)
+    def _():
+        for load in bank_loads:
+            load.wait()
+        for p in range(group):
+            @pl.when(p != blk % group)
+            def _():
+                for e in range(banks):
+                    b_copy(e, p).wait_recv()
+
+        @pl.loop(0, nb * nc)
+        def _(n):
+            b, j = n // nc, n % nc
+            start = pl.multiple_of(n * rc, rc)
+            xo = (n * rc) // own
             low = lax.dot_general(
-                piece, dnp[...], (((1,), (1,)), ((), ())), preferred_element_type=jnp.float32
+                xall[pl.ds(start, rc), :], dnp[...], (((1,), (1,)), ((), ())),
+                preferred_element_type=jnp.float32,
             )
-            part = jnp.dot(piece, wv[...], preferred_element_type=jnp.float32)
 
             @pl.when(xo == split)
             def _():
-                at = pl.ds(pl.multiple_of(b * rows + j * rc - xo * own, rc), rc)
-                lacc[at, :] = low
-                acc[at, :] = part
+                lacc[pl.ds(pl.multiple_of(n * rc - xo * own, rc), rc), :] = low
 
             @pl.when(xo != split)
             def _():
                 ls[pl.ds(start, rc), :] = low
-                xs[pl.ds(start, rc), :] = part.astype(xs.dtype)
-                for copy in x_pair(xo, b, j, split):
-                    copy.start()
-
-    def settle(i):
-        d, j, side, b, valid = place(i)
-        xo = (b * rows + j * rc) // own
-
-        @pl.when(valid & (i >= 0) & (i < steps) & (xo == split))
-        def _():
-            o = (b * rows + j * rc - xo * own) // rc
+                l_copy(xo, b, j, split).start()
+
+        @pl.loop(0, own // rc)
+        def _(o):
             at = pl.ds(pl.multiple_of(o * rc, rc), rc)
-            start = pl.multiple_of(b * rows + j * rc, rc)
+            n = split * (own // rc) + o
             low = lacc[at, :]
             for k in range(1, ns):
                 src = lax.rem(split + k, ns)
-                x_pair(xo, b, j, src, 1)[0].wait_recv()
+                l_copy(split, n // nc, n % nc, src).wait_recv()
                 low = low + lr[src, at, :]
-            lowx[blk, at, :] = (low * mtab[pl.ds(start, rc), :]).astype(lowx.dtype)
-            for k in range(1, nb):
-                g_copy(k, o).start()
-
-    @pl.loop(0, steps + 4)
-    def _(i):
-        arrive(i)
-        compute(i - 2)
-        settle(i - 4)
+            scale = mtab[pl.ds(pl.multiple_of(n * rc, rc), rc), :]
+            lowx[upper, at, :] = (low * scale).astype(lowx.dtype)
+
+        for k in range(1, nb):
+            g_copy(k, upper).start()
+
+    def from_far(h):
+        return jnp.logical_not(in_middle & (upper == h))
+
+    for h in range(2):
+        @pl.when(from_far(h))
+        def _():
+            g_copy(1, h).wait_recv()
+            for k in range(1, nu):
+                f_copy(k, h, sub).start()
+    for h in range(2):
+        @pl.when(from_far(h))
+        def _():
+            for k in range(1, nu):
+                f_copy(k, h, lax.rem(sub - k + nu, nu)).wait_recv()
 
     for k in range(1, ns):
         for e in range(up_banks):
@@ -276,20 +347,32 @@
                 device_id_type=MESH,
             ).wait_recv()
             value = value + xr[src, at, :].astype(jnp.float32)
-        for k in range(1, nb):
-            g_copy(k, o).wait_recv()
-        for p in range(nb):
-            value = value + jnp.dot(lowx[p, at, :], upp[p], preferred_element_type=jnp.float32)
+        for h in range(2):
+            value = value + jnp.dot(
+                lowx[h, at, :], upp[h * wide:(h + 1) * wide, :],
+                preferred_element_type=jnp.float32,
+            )
         o_ref[at, :] = value.astype(o_ref.dtype)
 
     for k in range(1, ns):
         for e in range(up_banks):
             u_copy(k, e, split).wait_send()
 
-    @pl.loop(0, own // rc)
-    def _(o):
+    @pl.when(in_middle)
+    def _():
         for k in range(1, nb):
-            g_copy(k, o).wait_send()
+            g_copy(k, upper).wait_send()
+
+    @pl.when(jnp.logical_not(in_middle))
+    def _():
+        for e in range(banks):
+            b_copy(e, blk % group).wait_send()
+
+    for h in range(2):
+        @pl.when(from_far(h))
+        def _():
+            for k in range(1, nu):
+                f_copy(k, h, sub).wait_send()
 
     @pl.loop(0, nb * nc)
     def _(n):
@@ -298,8 +381,11 @@
 
         @pl.when(xo != split)
         def _():
-            for copy in x_pair(xo, b, j, split):
-                copy.wait_send()
+            p_copy(xo, b, j, split).wait_send()
+
+            @pl.when(in_middle)
+            def _():
+                l_copy(xo, b, j, split).wait_send()
 
         @pl.when((b <= blk) & (blk < nb - 1))
         def _():
@@ -331,7 +417,7 @@
     banks, rank, _ = down_adapter_bank.shape
     up_banks = up_adapter_bank.shape[0]
     total = rollout_row_tenant.shape[0]
-    wide = -(-banks * rank // 128) * 128
+    wide = nb // 2 * banks * rank
     rc = CHUNK_ROWS
     chunks = total // rc
     dma = pltpu.SemaphoreType.DMA
@@ -349,7 +435,7 @@
             pltpu.VMEM((feats, cols), bf16),
             pltpu.VMEM((own, cols), bf16),
             pltpu.VMEM((wide, feats), bf16),
-            pltpu.VMEM((nb, wide, cols), bf16),
+            pltpu.VMEM((2 * wide, cols), bf16),
             pltpu.VMEM((total, wide), f32),
             pltpu.VMEM((own, cols), f32),
             pltpu.VMEM((own, wide), f32),
@@ -357,7 +443,7 @@
             pltpu.VMEM((total, wide), f32),
             pltpu.VMEM((ns, own, cols), bf16),
             pltpu.VMEM((ns, own, wide), f32),
-            pltpu.VMEM((nb, own, wide), bf16),
+            pltpu.VMEM((2, own, wide), bf16),
             dma((2 + banks + up_banks,)),
             dma,
             dma((2, chunks)),
@@ -370,8 +456,12 @@
             dma((ns, own // rc)),
             dma((chunks,)),
             dma((ns, own // rc)),
-            dma((nb - 1, own // rc)),
-            dma((nb - 1, own // rc)),
+            dma((nb - 1,)),
+            dma((2,)),
+            dma((nu - 1, 2)),
+            dma((nu - 1, 2)),
+            dma((banks,)),
+            dma((nb // 2, banks)),
         ],
         compiler_params=pltpu.CompilerParams(
             collective_id=0, has_side_effects=True

time: 60.1 us -> 51.6 us (0.86)
  Pallas kernels: 58 us -> 49.6 us
    pallas_call x1, Pallas kernels: 58 us -> 49.6 us  [shards(): pl.pallas_call(functools.partial(kernel, nb, ns, nu, rc), out_shape=jax.S...]
where the time goes in v3:
time: 51.6 us; the launch traced here: 51.5 us
  Pallas kernels  49.6 us (96%)
  local copies, waits for them, and re-layouts  1.87 us (4%)
    pallas_call x1, Pallas kernels, shards(): pl.pallas_call(functools.partial(kernel, nb, ns, nu, rc), out_shape=jax.S...  49.6 us
    unnamed x1, local copies, waits for them, and re-layouts  1.87 us

profile of v3, /device:TPU:0, one launch (start us, length us, event | category | flops | bytes accessed | tf_op | source)
XLA Modules:
  0.0 51.5 jit_solution(5991558927120217425)
XLA Ops:
  0.0 49.6 %shard_map.82 = bf16[256,1024]{1,0:T(8,128)(2,1)} custom-call(s32[4]{0:T(128)} %ent_ref.1, s32[4]{0:T(128)} %rank_ref.1, bf16[128,4096]{1,0:T(8,128)(2,1)} %x_ref.1, bf16[256,1024]{1,0:T(8,128)(2,1)} %r_ref.1, bf16[4096,1024]{1,0:T(8,128)(2,1)} %w_ref.1, bf16[1,64,4096]{2,1,0:T(8,128)(2,1)} %dn_ref.1, bf16[2,64,1024]{2,1,0:T(8,128)(2,1)} %up_ref.1, ...), custom_call_target="tpu_custom_call" | custom-call | tf_op jit(solution)/shard_map/pallas_call | solution.py:428
  49.6 1.9 %copy.10 = bf16[256,1024]{1,0:T(8,128)(2,1)} copy(bf16[256,1024]{1,0:T(8,128)(2,1)} %shard_map.82) | data formatting | bytes 1048576

commit v4 on v3

--- a/solution.py
+++ b/solution.py
@@ -8,6 +8,7 @@
 from jax.sharding import PartitionSpec as P
 
 CHUNK_ROWS = 64
+PARTS = 2
 MESH = pl.DeviceIdType.MESH
 
 
@@ -184,8 +185,10 @@
             device_id_type=MESH,
         )
 
-    def p_copy(*where):
-        return x_copy_of(xs, xr, xsend, xrecv, *where)
+    part_cols = cols // PARTS
+
+    def p_copy(h, *where):
+        return x_copy_of(xs.at[h], xr.at[h], xsend.at[h], xrecv.at[h], *where)
 
     def l_copy(*where):
         return x_copy_of(ls, lr, lsend, lrecv, *where)
@@ -252,17 +255,19 @@
             start = pl.multiple_of(b * rows + j * rc, rc)
             xo = (b * rows + j * rc) // own
             piece = xall[pl.ds(start, rc), :]
-            part = jnp.dot(piece, wv[...], preferred_element_type=jnp.float32)
-
-            @pl.when(xo == split)
-            def _():
-                at = pl.ds(pl.multiple_of(b * rows + j * rc - xo * own, rc), rc)
-                acc[at, :] = part
-
-            @pl.when(xo != split)
-            def _():
-                xs[pl.ds(start, rc), :] = part.astype(xs.dtype)
-                p_copy(xo, b, j, split).start()
+            for h in range(PARTS):
+                here = pl.ds(h * part_cols, part_cols)
+                part = jnp.dot(piece, wv[:, here], preferred_element_type=jnp.float32)
+
+                @pl.when(xo == split)
+                def _():
+                    at = pl.ds(pl.multiple_of(b * rows + j * rc - xo * own, rc), rc)
+                    acc[at, here] = part
+
+                @pl.when(xo != split)
+                def _():
+                    xs[h, pl.ds(start, rc), :] = part.astype(xs.dtype)
+                    p_copy(h, xo, b, j, split).start()
 
     @pl.loop(0, steps + 2)
     def _(i):
@@ -333,25 +338,24 @@
             u_copy(k, e, lax.rem(split - k + ns, ns)).wait_recv()
 
     @pl.loop(0, own // rc)
-    def _(o):
+    def _(n):
+        per = min(nc, own // rc)
+        o = jnp.where(upper == 0, n, (own // rc // per - 1 - n // per) * per + n % per)
         at = pl.ds(pl.multiple_of(o * rc, rc), rc)
         value = rv[at, :].astype(jnp.float32) + acc[at, :]
-        for k in range(1, ns):
-            src = lax.rem(split + k, ns)
-            pltpu.make_async_remote_copy(
-                src_ref=xs.at[at],
-                dst_ref=xr.at[src, at],
-                send_sem=xsend.at[o],
-                recv_sem=xrecv.at[src, o],
-                device_id={"split": src},
-                device_id_type=MESH,
-            ).wait_recv()
-            value = value + xr[src, at, :].astype(jnp.float32)
         for h in range(2):
             value = value + jnp.dot(
                 lowx[h, at, :], upp[h * wide:(h + 1) * wide, :],
                 preferred_element_type=jnp.float32,
             )
+        for k in range(1, ns):
+            src = lax.rem(split + k, ns)
+            n_all = split * (own // rc) + o
+            theirs = []
+            for h in range(PARTS):
+                p_copy(h, split, n_all // nc, n_all % nc, src).wait_recv()
+                theirs.append(xr[h, src, at, :].astype(jnp.float32))
+            value = value + jnp.concatenate(theirs, axis=1)
         o_ref[at, :] = value.astype(o_ref.dtype)
 
     for k in range(1, ns):
@@ -381,7 +385,8 @@
 
         @pl.when(xo != split)
         def _():
-            p_copy(xo, b, j, split).wait_send()
+            for h in range(PARTS):
+                p_copy(h, xo, b, j, split).wait_send()
 
             @pl.when(in_middle)
             def _():
@@ -439,9 +444,9 @@
             pltpu.VMEM((total, wide), f32),
             pltpu.VMEM((own, cols), f32),
             pltpu.VMEM((own, wide), f32),
-            pltpu.VMEM((total, cols), bf16),
+            pltpu.VMEM((PARTS, total, cols // PARTS), bf16),
             pltpu.VMEM((total, wide), f32),
-            pltpu.VMEM((ns, own, cols), bf16),
+            pltpu.VMEM((PARTS, ns, own, cols // PARTS), bf16),
             pltpu.VMEM((ns, own, wide), f32),
             pltpu.VMEM((2, own, wide), bf16),
             dma((2 + banks + up_banks,)),
@@ -452,8 +457,8 @@
             dma((nu - 1, chunks)),
             dma((ns - 1, up_banks)),
             dma((ns - 1, up_banks)),
-            dma((chunks,)),
-            dma((ns, own // rc)),
+            dma((PARTS, chunks)),
+            dma((PARTS, ns, own // rc)),
             dma((chunks,)),
             dma((ns, own // rc)),
             dma((nb - 1,)),

time: 51.6 us -> 51.2 us (level)
  no operation moved by 1% of the time
where the time goes in v4:
time: 51.2 us; the launch traced here: 51 us
  Pallas kernels  49.1 us (96%)
  local copies, waits for them, and re-layouts  1.87 us (4%)
    pallas_call x1, Pallas kernels, shards(): pl.pallas_call(functools.partial(kernel, nb, ns, nu, rc), out_shape=jax.S...  49.1 us
    unnamed x1, local copies, waits for them, and re-layouts  1.87 us

profile of v4, /device:TPU:0, one launch (start us, length us, event | category | flops | bytes accessed | tf_op | source)
XLA Modules:
  0.0 51.0 jit_solution(14501824209536749229)
XLA Ops:
  0.0 49.1 %shard_map.82 = bf16[256,1024]{1,0:T(8,128)(2,1)} custom-call(s32[4]{0:T(128)} %ent_ref.1, s32[4]{0:T(128)} %rank_ref.1, bf16[128,4096]{1,0:T(8,128)(2,1)} %x_ref.1, bf16[256,1024]{1,0:T(8,128)(2,1)} %r_ref.1, bf16[4096,1024]{1,0:T(8,128)(2,1)} %w_ref.1, bf16[1,64,4096]{2,1,0:T(8,128)(2,1)} %dn_ref.1, bf16[2,64,1024]{2,1,0:T(8,128)(2,1)} %up_ref.1, ...), custom_call_target="tpu_custom_call" | custom-call | tf_op jit(solution)/shard_map/pallas_call | solution.py:433
  49.2 1.9 %copy.10 = bf16[256,1024]{1,0:T(8,128)(2,1)} copy(bf16[256,1024]{1,0:T(8,128)(2,1)} %shard_map.82) | data formatting | bytes 1048576
